TPU v7x, 256 devices: a whole 4x4x8 slice. The times are simulated.
256 devices in a mesh: batch: 8 (over z), col: 32 (over y, x, core).
Axes of the slice: x: 4, y: 4, z: 8, core: 2. Of those that a mesh axis runs over, the one named last changes fastest.
Arguments:
- views: bfloat16 [2, 1024, 4096], P(None, 'batch', 'col'), may hold values from -132 to 132
- norm_scale_gain: float32 [4096], P('col'), may hold values from 0.5 to 1.5
- norm_shift_bias: float32 [4096], P('col'), may hold values from -3 to 3
- weight: bfloat16 [4096, 8192], P(None, 'col'), may hold values from -0.09375 to 0.09375
Outputs:
- loss: float32 [], replicated
- grad_weight: float32 [4096, 8192], P('batch', 'col')
- grad_gain: float32 [4096], P('col')
- grad_bias: float32 [4096], P('col')
- views_gradient: float32 [2, 1024, 4096], P(None, 'batch', 'col')
All inputs are finite; a program needn't handle non-finite values.
Results may differ from a plain program's by a relative error of at most 0.0027.
Values may be sent and summed in bfloat16 or wider, within the bound.
A program may use at most 64 MiB of HBM per device.

v0:
```python
import jax
import jax.numpy as jnp
from jax import lax
from jax.sharding import PartitionSpec as P

E = 8192
eps_norm = 1e-05
eps_std = 0.0001


def gelu_slope(preactivation):
    value, pullback = jax.vjp(lambda t: jax.nn.gelu(t, approximate=True), preactivation)
    return pullback(jnp.ones_like(value))[0]


def shards(views, norm_scale_gain, norm_shift_bias, weight):
    n_batch = lax.axis_size("batch")
    n_col = lax.axis_size("col")
    local_rows = views.shape[1]
    sample_count = local_rows * n_batch
    scale = sample_count * E / 128.0
    hidden_float = views.astype(jnp.float32)
    total = lax.psum(jnp.sum(hidden_float, axis=1), "batch")
    batch_average = total[:, None, :] / sample_count
    centred = hidden_float - batch_average
    spread = lax.psum(jnp.sum(centred * centred, axis=1), "batch")
    var = spread[:, None, :] / sample_count
    inverse_deviation = 1.0 / jnp.sqrt(var + eps_norm)
    normalised_input = (hidden_float - batch_average) * inverse_deviation
    preactivation = norm_scale_gain * normalised_input + norm_shift_bias
    act = jax.nn.gelu(preactivation, approximate=True).astype(jnp.bfloat16)
    act_full = lax.all_gather(act, "col", axis=2, tiled=True)
    z_local = jnp.einsum(
        "vrk,kj->vrj", act_full, weight, preferred_element_type=jnp.float32
    ).astype(jnp.bfloat16)
    z_all = lax.all_gather(z_local, "batch", axis=1, tiled=True)
    zf_all = z_all.astype(jnp.float32)
    zmean = jnp.mean(zf_all, axis=1, keepdims=True)
    zc_all = zf_all - zmean
    zvar = jnp.sum(zc_all * zc_all, axis=1, keepdims=True) / (sample_count - 1)
    std = jnp.sqrt(zvar + eps_std)
    zcb_all = zc_all.astype(jnp.bfloat16)
    offset = lax.axis_index("batch") * local_rows
    zc_loc = lax.dynamic_slice_in_dim(zc_all, offset, local_rows, 1)
    zcb_loc = zc_loc.astype(jnp.bfloat16)
    diag = jnp.sum(jnp.square(zcb_all.astype(jnp.float32)), axis=1, keepdims=True)
    kernel_part = jnp.einsum("vrj,vmj->vrm", zcb_loc, zcb_all, preferred_element_type=jnp.float32)
    kernel = lax.psum(kernel_part, "col")
    kernel_b = kernel.astype(jnp.bfloat16)
    denom = float((sample_count - 1) ** 2 * E)
    coef = 4.0 * scale / denom
    hinge_coef = 25.0 * scale / (2.0 * E * (sample_count - 1))
    mask = jnp.where(std < 1.0, 1.0, 0.0)
    moved = jnp.einsum("vrm,vmj->vrj", kernel_b, zcb_all, preferred_element_type=jnp.float32)
    g_cov = coef * (moved - zcb_loc.astype(jnp.float32) * diag)
    g_var = -hinge_coef * mask * zc_loc / std
    summed = g_cov + g_var
    col_total = lax.psum(jnp.sum(summed, axis=1), "batch")
    zf_loc = z_local.astype(jnp.float32)
    diff = zf_loc[0] - zf_loc[1]
    g_inv = 50.0 * scale / (sample_count * E) * diff
    dz = summed - col_total[:, None, :] / sample_count + jnp.stack([g_inv, -g_inv])
    dzb = dz.astype(jnp.bfloat16)
    inv_share = jnp.sum(diff * diff) / (sample_count * E)
    hinge_share = jnp.sum(jnp.maximum(1.0 - std, 0.0)) / (2 * E)
    block_share = jnp.sum(kernel * kernel) / denom
    diag_share = jnp.sum(diag * diag) / denom
    share = 25.0 * inv_share + (25.0 * hinge_share - diag_share) / n_batch + block_share / n_col
    loss = lax.psum(share, ("batch", "col"))
    d_act_t = lax.psum_scatter(
        jnp.einsum("kj,vrj->kvr", weight, dzb, preferred_element_type=jnp.float32),
        "col",
        scatter_dimension=0,
        tiled=True,
    )
    d_act = jnp.transpose(d_act_t, (1, 2, 0))
    grad_weight = lax.psum_scatter(
        jnp.einsum("vrk,vrj->kj", act_full, dzb, preferred_element_type=jnp.float32),
        "batch",
        scatter_dimension=0,
        tiled=True,
    )
    preactivation_gradient = d_act * gelu_slope(preactivation)
    bias_gradient_sum, gain_gradient_sum = lax.psum(
        (
            jnp.sum(preactivation_gradient, axis=1),
            jnp.sum(preactivation_gradient * normalised_input, axis=1),
        ),
        "batch",
    )
    grad_bias = jnp.sum(bias_gradient_sum, axis=0)
    grad_gain = jnp.sum(gain_gradient_sum, axis=0)
    views_gradient = (
        norm_scale_gain
        * (
            preactivation_gradient
            - bias_gradient_sum[:, None, :] / sample_count
            - normalised_input * gain_gradient_sum[:, None, :] / sample_count
        )
        * inverse_deviation
    )
    return (loss, grad_weight, grad_gain, grad_bias, views_gradient)


def solution(mesh):
    placed = (P(None, "batch", "col"), P("col"), P("col"), P(None, "col"))
    return jax.shard_map(
        shards,
        mesh=mesh,
        in_specs=placed,
        out_specs=(P(), P("batch", "col"), P("col"), P("col"), P(None, "batch", "col")),
        check_vma=False,
    )
```

profile of v0, /device:TPU:1, one launch (start us, length us, event | category | flops | bytes accessed | tf_op | source)
XLA Modules:
  0.0 430.3 jit_solution(8545685748164966906)
XLA Ops:
  7.2 0.0 copy-start
  7.2 0.0 all-gather.3.cloned.1.call-start
  7.2 1.0 convert_reduce_fusion.1
  8.2 17.3 %psum.49 = f32[2,128]{1,0:T(2,128)S(1)} all-reduce(f32[2,128]{1,0:T(2,128)S(1)} %convert_reduce_fusion.1), channel_id=1, replica_groups=mesh['batch'=8,'col'=32] {'batch'}, use_global_device_ids=true, to_apply=%region_1.0 | all-reduce | flops 256 | bytes 2048 | tf_op jit(solution)/shard_map/psum | solution.py:23
  25.5 0.9 fusion.32
  26.4 10.8 %psum.50 = f32[2,128]{1,0:T(2,128)S(1)} all-reduce(f32[2,128]{1,0:T(2,128)S(1)} %fusion.32), channel_id=1, replica_groups=mesh['batch'=8,'col'=32] {'batch'}, use_global_device_ids=true, to_apply=%region_3.0 | all-reduce | flops 256 | bytes 2048 | tf_op jit(solution)/shard_map/psum | solution.py:26
  37.2 1.6 fusion.25
  38.8 0.0 all-gather.3.cloned.1.call-update
  38.8 0.0 all-gather.5.cloned.1.call-start
  38.8 56.4 %all-gather.3.cloned.1.call-done = bf16[2,128,4096]{2,1,0:T(8,128)(2,1)} async-done(((bf16[2,128,128]{2,1,0:T(8,128)(2,1)}), bf16[2,128,4096]{2,1,0:T(8,128)(2,1)}) %all-gather.3.cloned.1.call-update) | async-done | bytes 2097168 | tf_op jit(solution)/shard_map/all_gather | solution.py:32
  95.2 0.0 copy-done
  95.2 3.0 fusion.42
  98.2 0.0 all-gather.5.cloned.1.call-update
  98.2 0.0 all-reduce.3.cloned.1.call-start
  98.2 32.8 %all-gather.5.cloned.1.call-done = bf16[2,1024,256]{2,1,0:T(8,128)(2,1)} async-done(((bf16[2,128,256]{2,1,0:T(8,128)(2,1)}), bf16[2,1024,256]{2,1,0:T(8,128)(2,1)}) %all-gather.5.cloned.1.call-update) | async-done | bytes 1048592 | tf_op jit(solution)/shard_map/all_gather | solution.py:36
  131.1 1.5 convert_reduce_fusion
  132.6 2.1 multiply_reduce_fusion
  134.7 1.3 copy-done.2
  136.0 0.0 copy-done.1
  136.0 1.5 fusion.10
  137.5 0.0 all-reduce.3.cloned.1.call-update
  137.5 0.0 reduce-scatter.5.cloned.1.call-start
  137.6 1.3 fusion.41
  138.8 1.3 fusion.37
  140.2 115.7 %all-reduce.3.cloned.1.call-done = f32[2,128,1024]{2,1,0:T(8,128)} async-done(((f32[2,128,1024]{2,1,0:T(8,128)}), f32[2,128,1024]{2,1,0:T(8,128)}) %all-reduce.3.cloned.1.call-update) | async-done | bytes 1048592 | tf_op jit(solution)/shard_map/psum | solution.py:48
  255.9 2.4 fusion.43
  258.3 13.7 %psum.53 = f32[2,256]{1,0:T(2,128)S(1)} all-reduce(f32[2,256]{1,0:T(2,128)S(1)} %get-tuple-element.23), channel_id=1, replica_groups=mesh['batch'=8,'col'=32] {'batch'}, use_global_device_ids=true, to_apply=%region_14.15 | all-reduce | flops 512 | bytes 4096 | tf_op jit(solution)/shard_map/psum | solution.py:58
  272.0 0.0 copy-done.5
  272.0 1.0 fusion.13
  272.9 2.7 convolution_bitcast_fusion
  275.7 0.0 reduce-scatter.5.cloned.1.call-update
  275.7 0.0 reduce-scatter.3.cloned.1.call-start
  275.7 4.3 convolution_bitcast_fusion.1
  280.0 0.0 reduce-scatter.3.cloned.1.call-update
  281.4 0.6 multiply_reduce_fusion.4
  282.7 0.0 copy-done.4
  282.7 0.9 multiply_reduce_fusion.2
  284.2 78.4 %psum.52 = f32[]{:T(128)} all-reduce(f32[]{:T(128)S(6)} %add.83), channel_id=1, replica_groups=mesh['batch'=8,'col'=32] {'batch','col'}, use_global_device_ids=true, to_apply=%region_12.13 | all-reduce | flops 1 | bytes 8 | tf_op jit(solution)/shard_map/psum | solution.py:69
  362.6 1.7 reduce-scatter.5.cloned.1.call-done
  364.4 0.0 copy-done.3
  364.4 0.0 copy-done.6
  364.4 0.0 copy-done.7
  364.4 1.0 fusion.39
  365.4 14.1 %all-reduce = (f32[2,128]{1,0:T(2,128)S(1)}, f32[2,128]{1,0:T(2,128)S(1)}) all-reduce(f32[2,128]{1,0:T(2,128)S(1)} %get-tuple-element.8, f32[2,128]{1,0:T(2,128)S(1)} %get-tuple-element.7), channel_id=1, replica_groups=mesh['batch'=8,'col'=32] {'batch'}, use_global_device_ids=true, to_apply=%region_18.19 | all-reduce | flops 512 | bytes 4096 | tf_op jit(solution)/shard_map/psum | solution.py:84
  379.5 0.5 reduce_sum.137
  380.1 0.5 broadcast_multiply_fusion.3
  380.6 0.7 fusion.31
  381.3 42.5 %reduce-scatter.3.cloned.1.call-done = f32[512,256]{1,0:T(8,128)} async-done(((f32[4096,256]{1,0:T(8,128)}), f32[512,256]{1,0:T(8,128)}) %reduce-scatter.3.cloned.1.call-update) | async-done | bytes 524304 | tf_op jit(solution)/shard_map/reduce_scatter | solution.py:77
  (11 shorter events, 0.0 us)
Async XLA Ops:
  7.2 88.0 %copy-start = (bf16[4096,256]{1,0:T(8,128)(2,1)S(1)}, bf16[4096,256]{1,0:T(8,128)(2,1)}, u32[]{:S(2)}) copy-start(bf16[4096,256]{1,0:T(8,128)(2,1)} %param.7) | copy-start | bytes 6291460
  7.2 88.0 %all-gather.3.cloned.1.call-start = ((), (), s32[]{:S(2)}) async-start(), calls=%async_computation.2 | async-start | bytes 2162688 | tf_op jit(solution)/shard_map/all_gather | solution.py:32
  38.8 92.3 %all-gather.5.cloned.1.call-start = ((), (), s32[]{:S(2)}) async-start(), calls=%async_computation.3 | async-start | bytes 1179648 | tf_op jit(solution)/shard_map/all_gather | solution.py:36
  98.2 157.7 %all-reduce.3.cloned.1.call-start = ((), (), s32[]{:S(2)}) async-start(), calls=%async_computation.4 | async-start | bytes 2097152 | tf_op jit(solution)/shard_map/psum | solution.py:48
  131.1 5.0 %copy-start.1 = (bf16[2,1024,256]{2,1,0:T(8,128)(2,1)S(1)}, bf16[2,1024,256]{2,1,0:T(8,128)(2,1)}, u32[]{:S(2)}) copy-start(bf16[2,1024,256]{2,1,0:T(8,128)(2,1)} %all-gather.5.cloned.1.call-done) | copy-start | bytes 3145732
  134.6 1.4 copy-start.2
  137.5 226.9 %reduce-scatter.5.cloned.1.call-start = ((), (), s32[]{:S(2)}) async-start(), calls=%async_computation.6 | async-start | bytes 4325376 | tf_op jit(solution)/shard_map/reduce_scatter | solution.py:70
  138.8 133.1 %copy-start.5 = (f32[1,128,256]{2,1,0:T(8,128)S(1)}, f32[1,128,256]{2,1,0:T(8,128)}, u32[]{:S(2)}) copy-start(f32[1,128,256]{2,1,0:T(8,128)} %get-tuple-element.13) | copy-start | bytes 393220
  275.7 148.1 %reduce-scatter.3.cloned.1.call-start = ((), (), s32[]{:S(2)}) async-start(), calls=%async_computation.5 | async-start | bytes 4718592 | tf_op jit(solution)/shard_map/reduce_scatter | solution.py:77
  280.0 2.7 copy-start.4
  280.0 84.3 %copy-start.3 = (bf16[2,128,128]{2,1,0:T(8,128)(2,1)S(1)}, bf16[2,128,128]{2,1,0:T(8,128)(2,1)}, u32[]{:S(2)}) copy-start(bf16[2,128,128]{2,1,0:T(8,128)(2,1)} %param.4) | copy-start | bytes 196612
  280.0 84.3 %copy-start.6 = (f32[128]{0:T(128)S(1)}, f32[128]{0:T(128)}, u32[]{:S(2)}) copy-start(f32[128]{0:T(128)} %param.5) | copy-start | bytes 1540
  280.0 84.3 %copy-start.7 = (f32[128]{0:T(128)S(1)}, f32[128]{0:T(128)}, u32[]{:S(2)}) copy-start(f32[128]{0:T(128)} %param.6) | copy-start | bytes 1540
Sparse Core Ops, SparseCore 0:
  38.9 56.2 all-gather.2
  98.3 32.7 all-gather.4
  137.6 118.2 all-reduce.2
  275.8 88.5 reduce-scatter.4
  367.3 56.3 reduce-scatter.2
where the time goes:
time: 431 us; the launch traced here: 430 us
  waiting for transfers between devices  249 us (58%)
  blocking collectives  134 us (31%)
  between operations  16.5 us (4%)
  other arithmetic  14.9 us (3%)
  matrix products  13.8 us (3%)
    psum x1, waiting for transfers between devices, shards(): kernel = lax.psum(kernel_part, 'col')  116 us
    psum x1, blocking collectives, shards(): loss = lax.psum(share, ('batch', 'col'))  78.4 us
    all_gather x1, waiting for transfers between devices, shards(): act_full = lax.all_gather(act, 'col', axis=2, tiled=True)  56.4 us
    reduce_scatter x1, waiting for transfers between devices, shards(): lax.psum_scatter(jnp.einsum('vrk,vrj->kj', act_full, dzb, preferred_eleme...  42.5 us
    all_gather x1, waiting for transfers between devices, shards(): z_all = lax.all_gather(z_local, 'batch', axis=1, tiled=True)  32.8 us
    psum x1, blocking collectives, shards(): total = lax.psum(jnp.sum(hidden_float, axis=1), 'batch')  17.3 us
    psum x1, blocking collectives, shards(): lax.psum((jnp.sum(preactivation_gradient, axis=1), jnp.sum(preactivation_...  14.1 us
    psum x1, blocking collectives, shards(): col_total = lax.psum(jnp.sum(summed, axis=1), 'batch')  13.7 us
  transfers between devices with their start and end apart: 5, of which 5 were waited for; matrix products, arithmetic and copies ran while one was open for 3% of the time, Pallas kernels for 0%

commit v1 on v0

--- a/solution.py
+++ b/solution.py
@@ -45,7 +45,7 @@
     zcb_loc = zc_loc.astype(jnp.bfloat16)
     diag = jnp.sum(jnp.square(zcb_all.astype(jnp.float32)), axis=1, keepdims=True)
     kernel_part = jnp.einsum("vrj,vmj->vrm", zcb_loc, zcb_all, preferred_element_type=jnp.float32)
-    kernel = lax.psum(kernel_part, "col")
+    kernel = jnp.sum(lax.all_gather(kernel_part, "col"), axis=0)
     kernel_b = kernel.astype(jnp.bfloat16)
     denom = float((sample_count - 1) ** 2 * E)
     coef = 4.0 * scale / denom

time: 431 us -> 448 us (1.039)
  other arithmetic: 14.9 us -> 27.7 us
  waiting for transfers between devices: 249 us -> 254 us
    all_gather x0 -> x1, waiting for transfers between devices: none -> 120 us  [shards(): kernel = jnp.sum(lax.all_gather(kernel_part, 'col'), axis=0)]
    psum x1 -> x0, waiting for transfers between devices: 116 us -> none  [shards(): kernel = lax.psum(kernel_part, 'col')]
    reduce_sum x0 -> x1, other arithmetic: none -> 12.8 us  [shards(): kernel = jnp.sum(lax.all_gather(kernel_part, 'col'), axis=0)]
  transfers between devices with their start and end apart: 5 -> 5, of which waited for: 5 -> 5; matrix products, arithmetic and copies ran while one was open for 3% -> 2% of each run, Pallas kernels for 0% -> 0%
where the time goes in v1:
time: 448 us; the launch traced here: 447 us
  waiting for transfers between devices  254 us (57%)
  blocking collectives  133 us (30%)
  other arithmetic  27.7 us (6%)
  between operations  16.5 us (4%)
  matrix products  13.8 us (3%)
    all_gather x1, waiting for transfers between devices, shards(): kernel = jnp.sum(lax.all_gather(kernel_part, 'col'), axis=0)  120 us
    psum x1, blocking collectives, shards(): loss = lax.psum(share, ('batch', 'col'))  77.1 us
    all_gather x1, waiting for transfers between devices, shards(): act_full = lax.all_gather(act, 'col', axis=2, tiled=True)  56.4 us
    reduce_scatter x1, waiting for transfers between devices, shards(): lax.psum_scatter(jnp.einsum('vrk,vrj->kj', act_full, dzb, preferred_eleme...  42.5 us
    all_gather x1, waiting for transfers between devices, shards(): z_all = lax.all_gather(z_local, 'batch', axis=1, tiled=True)  32.8 us
    psum x1, blocking collectives, shards(): total = lax.psum(jnp.sum(hidden_float, axis=1), 'batch')  17.3 us
    psum x1, blocking collectives, shards(): lax.psum((jnp.sum(preactivation_gradient, axis=1), jnp.sum(preactivation_...  14.2 us
    psum x1, blocking collectives, shards(): col_total = lax.psum(jnp.sum(summed, axis=1), 'batch')  13.8 us
  transfers between devices with their start and end apart: 5, of which 5 were waited for; matrix products, arithmetic and copies ran while one was open for 2% of the time, Pallas kernels for 0%

profile of v1, /device:TPU:1, one launch (start us, length us, event | category | flops | bytes accessed | tf_op | source)
XLA Modules:
  0.0 447.2 jit_solution(12151336873196752935)
XLA Ops:
  7.2 0.0 copy-start
  7.2 0.0 all-gather.5.cloned.1.call-start
  7.2 1.0 convert_reduce_fusion.1
  8.2 17.3 %psum.42 = f32[2,128]{1,0:T(2,128)S(1)} all-reduce(f32[2,128]{1,0:T(2,128)S(1)} %convert_reduce_fusion.1), channel_id=1, replica_groups=mesh['batch'=8,'col'=32] {'batch'}, use_global_device_ids=true, to_apply=%region_1.0 | all-reduce | flops 256 | bytes 2048 | tf_op jit(solution)/shard_map/psum | solution.py:23
  25.5 0.9 fusion.32
  26.4 10.8 %psum.43 = f32[2,128]{1,0:T(2,128)S(1)} all-reduce(f32[2,128]{1,0:T(2,128)S(1)} %fusion.32), channel_id=1, replica_groups=mesh['batch'=8,'col'=32] {'batch'}, use_global_device_ids=true, to_apply=%region_3.0 | all-reduce | flops 256 | bytes 2048 | tf_op jit(solution)/shard_map/psum | solution.py:26
  37.2 1.6 fusion.25
  38.8 0.0 all-gather.5.cloned.1.call-update
  38.8 0.0 all-gather.7.cloned.1.call-start
  38.8 56.4 %all-gather.5.cloned.1.call-done = bf16[2,128,4096]{2,1,0:T(8,128)(2,1)} async-done(((bf16[2,128,128]{2,1,0:T(8,128)(2,1)}), bf16[2,128,4096]{2,1,0:T(8,128)(2,1)}) %all-gather.5.cloned.1.call-update) | async-done | bytes 2097168 | tf_op jit(solution)/shard_map/all_gather | solution.py:32
  95.2 0.0 copy-done
  95.2 3.0 fusion.42
  98.2 0.0 all-gather.7.cloned.1.call-update
  98.2 0.0 all-gather.9.cloned.1.call-start
  98.2 32.8 %all-gather.7.cloned.1.call-done = bf16[2,1024,256]{2,1,0:T(8,128)(2,1)} async-done(((bf16[2,128,256]{2,1,0:T(8,128)(2,1)}), bf16[2,1024,256]{2,1,0:T(8,128)(2,1)}) %all-gather.7.cloned.1.call-update) | async-done | bytes 1048592 | tf_op jit(solution)/shard_map/all_gather | solution.py:36
  131.1 1.5 convert_reduce_fusion
  132.6 2.1 multiply_reduce_fusion
  134.7 1.4 copy-done.3
  136.0 0.0 copy-done.1
  136.0 1.5 fusion.10
  137.5 0.0 all-gather.9.cloned.1.call-update
  137.5 0.0 reduce-scatter.5.cloned.1.call-start
  137.6 1.3 fusion.41
  138.8 1.3 fusion.37
  140.1 120.2 %all-gather.9.cloned.1.call-done = f32[64,128,1024]{2,1,0:T(8,128)} async-done(((f32[2,128,1024]{2,1,0:T(8,128)}), f32[64,128,1024]{2,1,0:T(8,128)}) %all-gather.9.cloned.1.call-update) | async-done | bytes 33554448 | tf_op jit(solution)/shard_map/all_gather | solution.py:48
  260.3 12.8 %reduce_sum.143 = f32[2,128,1024]{2,1,0:T(8,128)} reduce(f32[32,2,128,1024]{3,2,1,0:T(8,128)} %bitcast.21, f32[]{:T(128)} %constant.24.clone.1), dimensions={0}, to_apply=%region_10.11 | reduce | flops 8126464 | bytes 34603012 | tf_op jit(solution)/shard_map/reduce_sum | solution.py:48
  273.2 2.4 fusion.43
  275.5 13.8 %psum.45 = f32[2,256]{1,0:T(2,128)S(1)} all-reduce(f32[2,256]{1,0:T(2,128)S(1)} %get-tuple-element.23), channel_id=1, replica_groups=mesh['batch'=8,'col'=32] {'batch'}, use_global_device_ids=true, to_apply=%region_14.15 | all-reduce | flops 512 | bytes 4096 | tf_op jit(solution)/shard_map/psum | solution.py:58
  289.4 0.0 copy-done.5
  289.4 1.0 fusion.13
  290.4 2.7 convolution_bitcast_fusion
  293.1 0.0 reduce-scatter.5.cloned.1.call-update
  293.1 0.0 reduce-scatter.3.cloned.1.call-start
  293.2 4.3 convolution_bitcast_fusion.1
  297.5 0.0 reduce-scatter.3.cloned.1.call-update
  298.9 0.6 multiply_reduce_fusion.4
  300.1 0.0 copy-done.2
  300.1 0.9 multiply_reduce_fusion.2
  301.7 77.1 %psum.44 = f32[]{:T(128)} all-reduce(f32[]{:T(128)S(6)} %add.81), channel_id=1, replica_groups=mesh['batch'=8,'col'=32] {'batch','col'}, use_global_device_ids=true, to_apply=%region_12.13 | all-reduce | flops 1 | bytes 8 | tf_op jit(solution)/shard_map/psum | solution.py:69
  378.8 2.4 reduce-scatter.5.cloned.1.call-done
  381.2 0.0 copy-done.4
  381.2 0.0 copy-done.6
  381.2 1.0 fusion.39
  382.2 14.2 %all-reduce = (f32[2,128]{1,0:T(2,128)S(1)}, f32[2,128]{1,0:T(2,128)S(1)}) all-reduce(f32[2,128]{1,0:T(2,128)S(1)} %get-tuple-element.8, f32[2,128]{1,0:T(2,128)S(1)} %get-tuple-element.7), channel_id=1, replica_groups=mesh['batch'=8,'col'=32] {'batch'}, use_global_device_ids=true, to_apply=%region_18.19 | all-reduce | flops 512 | bytes 4096 | tf_op jit(solution)/shard_map/psum | solution.py:84
  396.4 0.5 reduce_sum.147
  396.9 0.5 broadcast_multiply_fusion.3
  397.5 0.7 fusion.31
  398.2 42.5 %reduce-scatter.3.cloned.1.call-done = f32[512,256]{1,0:T(8,128)} async-done(((f32[4096,256]{1,0:T(8,128)}), f32[512,256]{1,0:T(8,128)}) %reduce-scatter.3.cloned.1.call-update) | async-done | bytes 524304 | tf_op jit(solution)/shard_map/reduce_scatter | solution.py:77
  (12 shorter events, 0.0 us)
Async XLA Ops:
  7.2 88.0 %copy-start = (bf16[4096,256]{1,0:T(8,128)(2,1)S(1)}, bf16[4096,256]{1,0:T(8,128)(2,1)}, u32[]{:S(2)}) copy-start(bf16[4096,256]{1,0:T(8,128)(2,1)} %param.7) | copy-start | bytes 6291460
  7.2 88.0 %all-gather.5.cloned.1.call-start = ((), (), s32[]{:S(2)}) async-start(), calls=%async_computation.2 | async-start | bytes 2162688 | tf_op jit(solution)/shard_map/all_gather | solution.py:32
  38.8 92.3 %all-gather.7.cloned.1.call-start = ((), (), s32[]{:S(2)}) async-start(), calls=%async_computation.3 | async-start | bytes 1179648 | tf_op jit(solution)/shard_map/all_gather | solution.py:36
  98.2 162.1 %all-gather.9.cloned.1.call-start = ((), (), s32[]{:S(2)}) async-start(), calls=%async_computation.6 | async-start | bytes 34603008 | tf_op jit(solution)/shard_map/all_gather | solution.py:48
  131.1 5.0 %copy-start.1 = (bf16[2,1024,256]{2,1,0:T(8,128)(2,1)S(1)}, bf16[2,1024,256]{2,1,0:T(8,128)(2,1)}, u32[]{:S(2)}) copy-start(bf16[2,1024,256]{2,1,0:T(8,128)(2,1)} %all-gather.7.cloned.1.call-done) | copy-start | bytes 3145732
  134.6 1.4 copy-start.3
  137.5 243.7 %reduce-scatter.5.cloned.1.call-start = ((), (), s32[]{:S(2)}) async-start(), calls=%async_computation.5 | async-start | bytes 4325376 | tf_op jit(solution)/shard_map/reduce_scatter | solution.py:70
  273.2 16.2 %copy-start.5 = (f32[1,128,256]{2,1,0:T(8,128)S(1)}, f32[1,128,256]{2,1,0:T(8,128)}, u32[]{:S(2)}) copy-start(f32[1,128,256]{2,1,0:T(8,128)} %get-tuple-element.13) | copy-start | bytes 393220
  293.1 147.6 %reduce-scatter.3.cloned.1.call-start = ((), (), s32[]{:S(2)}) async-start(), calls=%async_computation.4 | async-start | bytes 4718592 | tf_op jit(solution)/shard_map/reduce_scatter | solution.py:77
  297.5 2.7 copy-start.2
  297.5 83.7 %copy-start.4 = (bf16[2,128,128]{2,1,0:T(8,128)(2,1)S(1)}, bf16[2,128,128]{2,1,0:T(8,128)(2,1)}, u32[]{:S(2)}) copy-start(bf16[2,128,128]{2,1,0:T(8,128)(2,1)} %param.4) | copy-start | bytes 196612
  297.5 83.7 %copy-start.6 = (f32[128]{0:T(128)S(1)}, f32[128]{0:T(128)}, u32[]{:S(2)}) copy-start(f32[128]{0:T(128)} %param.5) | copy-start | bytes 1540
  297.5 83.7 %copy-start.7 = (f32[128]{0:T(128)S(1)}, f32[128]{0:T(128)}, u32[]{:S(2)}) copy-start(f32[128]{0:T(128)} %param.6) | copy-start | bytes 1540
Sparse Core Ops, SparseCore 0:
  38.9 56.2 all-gather.4
  98.3 32.7 all-gather.6
  137.6 122.6 all-gather.8
  293.2 87.8 reduce-scatter.4
  384.3 56.3 reduce-scatter.2
